TPU v7x, 256 devices: a whole 4x4x8 slice. The times are simulated.
256 devices in a mesh: row: 16 (over y, z_lo), col: 16 (over z_hi, x, core).
Axes of the slice: x: 4, y: 4, z: 8 (z_hi: 2, z_lo: 4; z = z_hi * 4 + z_lo), core: 2. Of those that a mesh axis runs over, the one named last changes fastest.
Arguments:
- laplacian: float32 [23040, 23040], P('row', 'col'), may hold values from -1 to 1.12, as said below
- block: float32 [23040, 256], P(('row', 'col')), may hold values from -6 to 6
- bounds: float32 [2], replicated, may hold values from 0.25 to 2.1, as said below
Outputs:
- filtered: float32 [23040, 256], P(('row', 'col'))
- rayleigh: float32 [256, 256], replicated
Inputs may be any that keep to these rules, and one draw needn't show every extreme that they name: laplacian is symmetric; its diagonal entries lie in 0.88 to 1.12 and its other entries have magnitude at most 1.14 / sqrt(23040). bounds[0] lies in 0.25 to 0.40 and bounds[1] in 1.95 to 2.10.
All inputs are finite; a program needn't handle non-finite values.
Results may differ from a plain program's by a relative error of at most 0.00025.
Values sent between devices are 32-bit elements; how exact they have to be, the bound alone decides.
A program may use at most 64 MiB of HBM per device.

v0:
```python
import jax
import jax.numpy as jnp
from jax import lax
from jax.sharding import PartitionSpec as P


def relayout(panel_rows, row_index, col_index, tile_rows, tile_cols):
    offset = col_index * tile_cols - row_index * tile_rows
    zeros_pad = jnp.zeros((tile_cols, panel_rows.shape[1]), jnp.float32)
    padded = jnp.concatenate([zeros_pad, panel_rows, zeros_pad], axis=0)
    start_row = jnp.clip(offset + tile_cols, 0, tile_rows + tile_cols)
    sliced = lax.dynamic_slice_in_dim(padded, start_row, tile_cols, 0)
    target = offset + lax.broadcasted_iota(jnp.int32, (tile_cols, 1), 0)
    inside = (target >= 0) & (target < tile_rows)
    return jnp.where(inside, sliced, 0.0)


def body(laplacian, block, bounds):
    row_index = lax.axis_index("row")
    col_index = lax.axis_index("col")
    tile_rows, tile_cols = laplacian.shape
    lower_bound = bounds[0]
    upper_bound = bounds[1]
    center = (upper_bound + lower_bound) * 0.5
    half_width = (upper_bound - lower_bound) * 0.5
    factor_two = 2.0 / half_width
    global_rows = row_index * tile_rows + lax.broadcasted_iota(jnp.int32, (tile_rows, tile_cols), 0)
    global_cols = col_index * tile_cols + lax.broadcasted_iota(jnp.int32, (tile_rows, tile_cols), 1)
    shifted = laplacian - center * (global_rows == global_cols).astype(jnp.float32)

    def through_columns(panel_rows):
        return lax.dot_general(
            shifted,
            panel_rows,
            (((0,), (0,)), ((), ())),
            precision=lax.Precision.HIGHEST,
            preferred_element_type=jnp.float32,
        )

    def through_rows(panel_cols):
        return jnp.dot(
            shifted, panel_cols, precision=lax.Precision.HIGHEST, preferred_element_type=jnp.float32
        )

    def gather_rows(values):
        return lax.all_gather(values, "col", axis=0, tiled=True)

    def gather_cols(values):
        return lax.all_gather(values, "row", axis=0, tiled=True)

    def column_sum(values):
        return lax.psum_scatter(values, "row", scatter_dimension=0, tiled=True)

    def row_sum(values):
        return lax.psum_scatter(values, "col", scatter_dimension=0, tiled=True)

    filter_one = column_sum(through_columns(gather_rows(block))) / half_width
    filter_two = factor_two * row_sum(through_rows(gather_cols(filter_one))) - block
    filter_three = factor_two * column_sum(through_columns(gather_rows(filter_two))) - filter_one
    filter_four = factor_two * row_sum(through_rows(gather_cols(filter_three))) - filter_two
    panel_four = gather_rows(filter_four)
    dims_inner = (((0,), (0,)), ((), ()))
    image_piece, moved_piece = (
        lax.psum_scatter(through_columns(panel_four), "row", scatter_dimension=0, tiled=True),
        lax.psum_scatter(
            relayout(panel_four, row_index, col_index, tile_rows, tile_cols),
            "row",
            scatter_dimension=0,
            tiled=True,
        ),
    )
    gram_part = lax.dot_general(
        moved_piece,
        moved_piece,
        dims_inner,
        precision=lax.Precision.HIGHEST,
        preferred_element_type=jnp.float32,
    )
    image_part = lax.dot_general(
        moved_piece,
        image_piece,
        dims_inner,
        precision=lax.Precision.HIGHEST,
        preferred_element_type=jnp.float32,
    )
    gram, projected = lax.psum((gram_part, image_part), ("row", "col"))
    projected = projected + center * gram
    projected = (projected + projected.T) * 0.5
    factor = jnp.linalg.cholesky(gram)
    first_solve = jax.scipy.linalg.solve_triangular(factor, projected, lower=True)
    rayleigh = jax.scipy.linalg.solve_triangular(factor, first_solve.T, lower=True)
    return (filter_four, rayleigh)


def solution(mesh):
    placed = (P("row", "col"), P(("row", "col"), None), P())
    return jax.shard_map(
        body, mesh=mesh, in_specs=placed, out_specs=(P(("row", "col"), None), P()), check_vma=False
    )
```

profile of v0, /device:TPU:2, one launch (start us, length us, event | category | flops | bytes accessed | tf_op | source)
XLA Modules:
  0.0 1090.3 jit_solution(2360731310481953332)
XLA Ops:
  7.2 0.7 all-gather.11.cloned.1.call-update
  8.0 1.3 fusion.44
  10.6 61.9 %all-gather.11.cloned.1.call-done = f32[16,90,256]{2,1,0:T(8,128)} async-done(((f32[1,90,256]{2,1,0:T(8,128)}), f32[16,90,256]{2,1,0:T(8,128)}) %all-gather.11.cloned.1.call-update) | async-done | bytes 1474576 | tf_op jit(solution)/shard_map/all_gather | solution.py:46
  72.5 1.5 reshape.61
  74.0 17.9 %fusion.41 = f32[1440,256]{1,0:T(8,128)S(1)} fusion(f32[1440,256]{1,0:T(8,128)S(1)} %reshape.61, f32[1440,1440]{1,0:T(8,128)} %param.5, f32[]{:T(128)} %bitcast.1, s32[1440]{0:T(1024)S(1)} %get-tuple-element.45, s32[1440]{0:T(1024)S(1)} %get-tuple-element.46), kind=kOutput, calls=%fused_computation.71 | convolution fusion | flops 6376320000 | bytes 11255044 | tf_op jit(solution)/shard_map/dot_general | solution.py:32
  91.8 55.3 %fusion = f32[96,256]{1,0:T(8,128)S(1)} fusion(f32[1440,256]{1,0:T(8,128)S(1)} %fusion.41), kind=kCustom, calls=%all-reduce-scatter | all-reduce-scatter fusion | flops 393217 | bytes 1573888
  147.1 1.3 collective-permute-start
  149.7 0.6 dynamic-slice.19
  151.3 0.7 fusion.30
  151.9 0.3 all-gather.15.cloned.1.call-start
  152.2 80.0 %all-gather.13.cloned.1.call-done = f32[16,90,256]{2,1,0:T(8,128)} async-done(((f32[1,90,256]{2,1,0:T(8,128)}), f32[16,90,256]{2,1,0:T(8,128)}) %all-gather.13.cloned.1.call-update) | async-done | bytes 1474576 | tf_op jit(solution)/shard_map/all_gather | solution.py:49
  232.3 1.5 reshape.63
  233.8 10.1 fusion.40
  243.9 48.1 %fusion.1 = f32[96,256]{1,0:T(8,128)S(1)} fusion(f32[1440,256]{1,0:T(8,128)S(1)} %fusion.40), kind=kCustom, calls=%all-reduce-scatter.1 | all-reduce-scatter fusion | flops 393217 | bytes 1573888
  292.0 1.9 collective-permute-start.1
  294.0 0.6 dynamic-slice.23
  295.2 2.7 collective-permute-done.1
  298.2 0.7 fusion.31
  298.9 66.9 %all-gather.15.cloned.1.call-done = f32[16,90,256]{2,1,0:T(8,128)} async-done(((f32[1,90,256]{2,1,0:T(8,128)}), f32[16,90,256]{2,1,0:T(8,128)}) %all-gather.15.cloned.1.call-update) | async-done | bytes 1474576 | tf_op jit(solution)/shard_map/all_gather | solution.py:46
  365.9 1.5 reshape.65
  367.4 17.9 %fusion.39 = f32[1440,256]{1,0:T(8,128)S(1)} fusion(f32[1440,256]{1,0:T(8,128)S(1)} %reshape.65, f32[1440,1440]{1,0:T(8,128)} %param.5, f32[]{:T(128)} %bitcast.1, s32[1440]{0:T(1024)S(1)} %get-tuple-element.45, s32[1440]{0:T(1024)S(1)} %get-tuple-element.46), kind=kOutput, calls=%fused_computation.69 | convolution fusion | flops 6376320000 | bytes 11255044 | tf_op jit(solution)/shard_map/dot_general | solution.py:32
  385.2 55.2 %fusion.2 = f32[96,256]{1,0:T(8,128)S(1)} fusion(f32[1440,256]{1,0:T(8,128)S(1)} %fusion.39), kind=kCustom, calls=%all-reduce-scatter.2 | all-reduce-scatter fusion | flops 393217 | bytes 1573888
  440.4 1.3 collective-permute-start.2
  441.7 2.2 collective-permute-done.2
  444.2 0.7 fusion.18
  444.9 10.4 all-gather.19.cloned.1.call-start
  455.3 70.4 %all-gather.17.cloned.1.call-done = f32[16,90,256]{2,1,0:T(8,128)} async-done(((f32[1,90,256]{2,1,0:T(8,128)}), f32[16,90,256]{2,1,0:T(8,128)}) %all-gather.17.cloned.1.call-update) | async-done | bytes 1474576 | tf_op jit(solution)/shard_map/all_gather | solution.py:49
  525.7 1.5 reshape.67
  527.1 10.1 fusion.38
  537.2 48.0 %fusion.3 = f32[96,256]{1,0:T(8,128)S(1)} fusion(f32[1440,256]{1,0:T(8,128)S(1)} %fusion.38), kind=kCustom, calls=%all-reduce-scatter.3 | all-reduce-scatter fusion | flops 393217 | bytes 1573888
  585.2 1.9 collective-permute-start.3
  587.2 4.0 collective-permute-done.3
  591.4 0.7 fusion.16
  592.2 66.9 %all-gather.19.cloned.1.call-done = f32[16,90,256]{2,1,0:T(8,128)} async-done(((f32[1,90,256]{2,1,0:T(8,128)}), f32[16,90,256]{2,1,0:T(8,128)}) %all-gather.19.cloned.1.call-update) | async-done | bytes 1474576 | tf_op jit(solution)/shard_map/all_gather | solution.py:46
  659.1 1.5 reshape.69
  660.6 19.0 %fusion.37 = f32[1440,256]{1,0:T(8,128)} fusion(f32[1440,256]{1,0:T(8,128)S(1)} %reshape.69, f32[1440,1440]{1,0:T(8,128)} %param.5, f32[]{:T(128)} %bitcast.1, s32[1440]{0:T(1024)S(1)} %get-tuple-element.45, s32[1440]{0:T(1024)S(1)} %get-tuple-element.46), kind=kOutput, calls=%fused_computation.67 | convolution fusion | flops 6376320000 | bytes 11255044 | tf_op jit(solution)/shard_map/dot_general | solution.py:32
  679.7 0.8 fusion.8
  680.5 74.2 %fusion.42 = (f32[96,256]{1,0:T(8,128)S(1)}, f32[96,256]{1,0:T(8,128)S(1)}) fusion(f32[1440,256]{1,0:T(8,128)} %fusion.37, f32[1440,256]{1,0:T(8,128)S(1)} %fusion.8), kind=kCustom, calls=%all-reduce-scatter.6 | all-reduce-scatter fusion | flops 786433 | bytes 3146752
  754.7 1.3 collective-permute-start.4
  756.0 1.5 collective-permute-start.5
  757.5 0.7 collective-permute-done.4
  758.4 1.1 fusion.21
  759.8 1.1 fusion.14
  761.0 256.2 %all-reduce.17.cloned.1.call-done = (f32[256,256]{0,1:T(8,128)}, f32[256,256]{0,1:T(8,128)}) async-done(((f32[256,256]{0,1:T(8,128)}, f32[256,256]{0,1:T(8,128)}), (f32[256,256]{0,1:T(8,128)}, f32[256,256]{0,1:T(8,128)})) %all-reduce.17.cloned.1.call-update) | async-done | bytes 524304 | tf_op jit(solution)/shard_map/psum | solution.py:86
  1017.2 1.1 copy.16
  1018.3 1.1 bitcast_add_fusion.1
  1019.6 11.7 %cholesky.50 = f32[128,128]{1,0:T(8,128)S(1)} custom-call(f32[128,128]{1,0:T(8,128)S(1)} %cholesky.118), custom_call_target="Cholesky" | custom-call | tf_op jit(solution)/shard_map/jit(cholesky)/cholesky | solution.py:89
  1031.4 9.8 custom-call.14
  1041.4 0.3 convolution_subtract_fusion.2
  1041.7 11.7 %cholesky.105 = f32[128,128]{1,0:T(8,128)S(1)} custom-call(f32[128,128]{1,0:T(8,128)S(1)} %convolution_subtract_fusion.2), custom_call_target="Cholesky" | custom-call | tf_op jit(solution)/shard_map/jit(cholesky)/cholesky | solution.py:89
  1053.4 0.7 compare_reduce_fusion
  1054.1 0.6 compare_reduce_fusion.1
  1056.2 4.1 while.4
  1056.2 0.6 fusion.57
  1056.8 1.4 bitcast_dynamic-update-slice_fusion.2
  1058.2 0.6 fusion.57
  1058.8 1.4 bitcast_dynamic-update-slice_fusion.2
  1060.3 19.9 %custom-call.17 = f32[2,128,128]{1,2,0:T(8,128)S(1)} custom-call(f32[2,128,128]{2,1,0:T(8,128)S(1)} %get-tuple-element.18), custom_call_target="InvertDiagBlocksLowerTriangular" | custom-call | tf_op jit(solution)/shard_map/jit(_solve_triangular)/triangular_solve | solution.py:91
  1080.4 0.3 fusion.12
  1080.9 0.3 fusion.27
  1081.3 0.3 fusion.10
  1081.6 0.4 convolution_subtract_fusion
  1082.0 0.3 fusion.26
  1082.3 0.7 pad_maximum_fusion
  (49 shorter events, 3.0 us)
Async XLA Ops:
  7.2 65.3 %all-gather.11.cloned.1.call-start = ((), (), s32[]{:S(2)}) async-start(), calls=%async_computation | async-start | bytes 1671168 | tf_op jit(solution)/shard_map/all_gather | solution.py:46
  7.9 224.4 %all-gather.13.cloned.1.call-start = ((), (), s32[]{:S(2)}) async-start(), calls=%async_computation.1 | async-start | bytes 1671168 | tf_op jit(solution)/shard_map/all_gather | solution.py:49
  91.8 57.9 %copy-start.2 = (u32[256]{0:T(256)S(1)}, u32[256]{0:T(256)}, u32[]{:S(2)}) copy-start(u32[256]{0:T(256)} %constant.130) | copy-start | bytes 3076
  147.1 3.9 collective-permute-start
  151.9 213.9 %all-gather.15.cloned.1.call-start = ((), (), s32[]{:S(2)}) async-start(), calls=%async_computation.2 | async-start | bytes 1671168 | tf_op jit(solution)/shard_map/all_gather | solution.py:46
  243.8 50.1 %copy-start.1 = (u32[256]{0:T(256)S(1)}, u32[256]{0:T(256)}, u32[]{:S(2)}) copy-start(u32[256]{0:T(256)} %constant.134) | copy-start | bytes 3076
  243.9 54.3 %copy-start = (f32[90,256]{1,0:T(8,128)S(1)}, f32[90,256]{1,0:T(8,128)}, u32[]{:S(2)}) copy-start(f32[90,256]{1,0:T(8,128)} %param.6) | copy-start | bytes 276484
  292.0 5.9 collective-permute-start.1
  298.9 226.8 %all-gather.17.cloned.1.call-start = ((), (), s32[]{:S(2)}) async-start(), calls=%async_computation.3 | async-start | bytes 1671168 | tf_op jit(solution)/shard_map/all_gather | solution.py:49
  440.4 3.5 collective-permute-start.2
  444.9 214.2 %all-gather.19.cloned.1.call-start = ((), (), s32[]{:S(2)}) async-start(), calls=%async_computation.4 | async-start | bytes 1671168 | tf_op jit(solution)/shard_map/all_gather | solution.py:46
  585.2 5.9 collective-permute-start.3
  592.1 425.1 %all-reduce.17.cloned.1.call-start = ((), (), s32[]{:S(2)}) async-start(), calls=%async_computation.5 | async-start | bytes 1048576 | tf_op jit(solution)/shard_map/psum | solution.py:86
  754.7 3.5 collective-permute-start.4
  756.0 3.6 collective-permute-start.5
Sparse Core Ops, SparseCore 0:
  10.7 61.7 all-gather.10
  152.1 80.1 all-gather.12
  299.0 66.7 all-gather.14
  445.0 80.5 all-gather.16
  592.3 66.7 all-gather.18
  761.1 256.0 all-reduce.16
where the time goes:
time: 1100 us; the launch traced here: 1090 us
  waiting for transfers between devices  613 us (56%)
  blocking collectives  281 us (26%)
  matrix products  79.5 us (7%)
  other arithmetic  60 us (5%)
  between operations  20.4 us (2%)
  starting transfers between devices  20.1 us (2%)
  local copies, waits for them, and re-layouts  17.1 us (2%)
    unnamed x5, blocking collectives  281 us
    psum x1, waiting for transfers between devices, body(): gram, projected = lax.psum((gram_part, image_part), ('row', 'col'))  256 us
    all_gather x3, waiting for transfers between devices, gather_rows(): return lax.all_gather(values, 'col', axis=0, tiled=True)  196 us
    all_gather x2, waiting for transfers between devices, gather_cols(): return lax.all_gather(values, 'row', axis=0, tiled=True)  150 us
    dot_general x3, matrix products, through_columns(): lax.dot_general(shifted, panel_rows, (((0,), (0,)), ((), ())), precision=...  54.7 us
    another operation x7, other arithmetic, body(): factor = jnp.linalg.cholesky(gram)  34.6 us
  transfers between devices with their start and end apart: 12, of which 10 were waited for; matrix products, arithmetic and copies ran while one was open for 0% of the time, Pallas kernels for 0%

commit v1 on v0

--- a/solution.py
+++ b/solution.py
@@ -43,7 +43,9 @@
         )
 
     def gather_rows(values):
-        return lax.all_gather(values, "col", axis=0, tiled=True)
+        return jnp.concatenate(
+            lax.all_to_all(jnp.stack([values] * lax.axis_size("col")), "col", 0, 0), axis=0
+        )
 
     def gather_cols(values):
         return lax.all_gather(values, "row", axis=0, tiled=True)

time: 1100 us -> 1060 us (0.964)
  waiting for transfers between devices: 613 us -> 493 us
  blocking collectives: 281 us -> 349 us
  starting transfers between devices: 20.1 us -> 39.8 us
    all_gather x3 -> x0, waiting for transfers between devices: 196 us -> none  [gather_rows(): return lax.all_gather(values, 'col', axis=0, tiled=True)]
    all_to_all x0 -> x2, waiting for transfers between devices: none -> 55.8 us  [gather_rows(): lax.all_to_all(jnp.stack([values] * lax.axis_size('col')), 'col', 0, 0)]
    all_to_all x0 -> x1, blocking collectives: none -> 53.3 us  [gather_rows(): lax.all_to_all(jnp.stack([values] * lax.axis_size('col')), 'col', 0, 0)]
    all_to_all x0 -> x2, starting transfers between devices: none -> 29.6 us  [gather_rows(): lax.all_to_all(jnp.stack([values] * lax.axis_size('col')), 'col', 0, 0)]
    all_gather x2, waiting for transfers between devices: 150 us -> 170 us  [gather_cols(): return lax.all_gather(values, 'row', axis=0, tiled=True)]
    unnamed x5, blocking collectives: 281 us -> 296 us
  transfers between devices with their start and end apart: 12 -> 11, of which waited for: 10 -> 9; matrix products, arithmetic and copies ran while one was open for 0% -> 0% of each run, Pallas kernels for 0% -> 0%
where the time goes in v1:
time: 1060 us
  waiting for transfers between devices  493 us (47%)
  blocking collectives  349 us (33%)
  matrix products  79.4 us (7%)
  other arithmetic  58.6 us (6%)
  starting transfers between devices  39.8 us (4%)
  between operations  19.7 us (2%)
  local copies, waits for them, and re-layouts  15.8 us (1%)
    unnamed x5, blocking collectives  296 us
    psum x1, waiting for transfers between devices, body(): gram, projected = lax.psum((gram_part, image_part), ('row', 'col'))  257 us
    all_gather x2, waiting for transfers between devices, gather_cols(): return lax.all_gather(values, 'row', axis=0, tiled=True)  170 us
    all_to_all x2, waiting for transfers between devices, gather_rows(): lax.all_to_all(jnp.stack([values] * lax.axis_size('col')), 'col', 0, 0)  55.8 us
    dot_general x3, matrix products, through_columns(): lax.dot_general(shifted, panel_rows, (((0,), (0,)), ((), ())), precision=...  54.7 us
    all_to_all x1, blocking collectives, gather_rows(): lax.all_to_all(jnp.stack([values] * lax.axis_size('col')), 'col', 0, 0)  53.3 us
    another operation x7, other arithmetic, body(): factor = jnp.linalg.cholesky(gram)  34.6 us
    all_to_all x2, starting transfers between devices, gather_rows(): lax.all_to_all(jnp.stack([values] * lax.axis_size('col')), 'col', 0, 0)  29.6 us
  transfers between devices with their start and end apart: 11, of which 9 were waited for; matrix products, arithmetic and copies ran while one was open for 0% of the time, Pallas kernels for 0%

profile of v1, /device:TPU:2, one launch (start us, length us, event | category | flops | bytes accessed | tf_op | source)
XLA Modules:
  0.0 1055.4 jit_solution(17470741312867040194)
XLA Ops:
  7.2 2.2 stack.6
  9.4 11.6 %all-to-all-start = ((f32[16,90,256]{2,1,0:T(8,128)}), f32[16,90,256]{2,1,0:T(8,128)S(1)}, u32[]{:S(2)}, u32[]{:S(2)}) async-start(f32[16,90,256]{2,1,0:T(8,128)} %stack.6), calls=%async_computation | async-start | bytes 3145728 | tf_op jit(solution)/shard_map/all_to_all | solution.py:47
  21.0 0.6 fusion.43
  22.9 21.2 %all-to-all-done = f32[16,90,256]{2,1,0:T(8,128)S(1)} async-done(((f32[16,90,256]{2,1,0:T(8,128)}), f32[16,90,256]{2,1,0:T(8,128)S(1)}, u32[]{:S(2)}, u32[]{:S(2)}) %all-to-all-start) | async-done | bytes 1474592 | tf_op jit(solution)/shard_map/all_to_all | solution.py:47
  44.3 17.9 %fusion.40 = f32[1440,256]{1,0:T(8,128)S(1)} fusion(f32[1440,256]{1,0:T(8,128)S(1)} %reshape.53, f32[1440,1440]{1,0:T(8,128)} %param.5, f32[]{:T(128)} %bitcast.1, s32[1440]{0:T(1024)S(1)} %get-tuple-element.45, s32[1440]{0:T(1024)S(1)} %get-tuple-element.46), kind=kOutput, calls=%fused_computation.70 | convolution fusion | flops 6376320000 | bytes 11255044 | tf_op jit(solution)/shard_map/dot_general | solution.py:32
  62.1 69.7 %fusion = f32[96,256]{1,0:T(8,128)S(1)} fusion(f32[1440,256]{1,0:T(8,128)S(1)} %fusion.40), kind=kCustom, calls=%all-reduce-scatter | all-reduce-scatter fusion | flops 393217 | bytes 1573888
  131.8 1.3 collective-permute-start
  134.4 0.6 dynamic-slice.19
  135.7 0.3 concatenate.7
  136.0 0.7 fusion.30
  136.9 84.2 %all-gather.5.cloned.1.call-done = f32[16,90,256]{2,1,0:T(8,128)} async-done(((f32[1,90,256]{2,1,0:T(8,128)}), f32[16,90,256]{2,1,0:T(8,128)}) %all-gather.5.cloned.1.call-update) | async-done | bytes 1474576 | tf_op jit(solution)/shard_map/all_gather | solution.py:51
  221.1 1.5 reshape.79
  222.6 10.1 fusion.39
  232.7 48.1 %fusion.1 = f32[96,256]{1,0:T(8,128)S(1)} fusion(f32[1440,256]{1,0:T(8,128)S(1)} %fusion.39), kind=kCustom, calls=%all-reduce-scatter.1 | all-reduce-scatter fusion | flops 393217 | bytes 1573888
  280.8 1.9 collective-permute-start.1
  282.8 0.6 dynamic-slice.23
  284.1 2.7 collective-permute-done.1
  287.2 53.3 %all_to_all.15 = f32[16,90,256]{2,1,0:T(8,128)S(1)} all-to-all(f32[16,90,256]{2,1,0:T(8,128)S(1)} %stack.7), channel_id=1, replica_groups=mesh['row'=16,'col'=16] {'col'}, dimensions={0} | all-to-all | bytes 2949120 | tf_op jit(solution)/shard_map/all_to_all | solution.py:47
  340.7 17.9 %fusion.38 = f32[1440,256]{1,0:T(8,128)S(1)} fusion(f32[1440,256]{1,0:T(8,128)S(1)} %reshape.54, f32[1440,1440]{1,0:T(8,128)} %param.5, f32[]{:T(128)} %bitcast.1, s32[1440]{0:T(1024)S(1)} %get-tuple-element.45, s32[1440]{0:T(1024)S(1)} %get-tuple-element.46), kind=kOutput, calls=%fused_computation.68 | convolution fusion | flops 6376320000 | bytes 11255044 | tf_op jit(solution)/shard_map/dot_general | solution.py:32
  358.6 54.4 %fusion.2 = f32[96,256]{1,0:T(8,128)S(1)} fusion(f32[1440,256]{1,0:T(8,128)S(1)} %fusion.38), kind=kCustom, calls=%all-reduce-scatter.2 | all-reduce-scatter fusion | flops 393217 | bytes 1573888
  413.0 1.6 collective-permute-start.2
  414.5 1.9 collective-permute-done.2
  416.7 0.7 fusion.18
  417.4 86.0 %all-gather.7.cloned.1.call-done = f32[16,90,256]{2,1,0:T(8,128)} async-done(((f32[1,90,256]{2,1,0:T(8,128)}), f32[16,90,256]{2,1,0:T(8,128)}) %all-gather.7.cloned.1.call-update) | async-done | bytes 1474576 | tf_op jit(solution)/shard_map/all_gather | solution.py:51
  503.5 1.5 reshape.81
  504.9 10.1 fusion.37
  515.0 48.0 %fusion.3 = f32[96,256]{1,0:T(8,128)S(1)} fusion(f32[1440,256]{1,0:T(8,128)S(1)} %fusion.37), kind=kCustom, calls=%all-reduce-scatter.3 | all-reduce-scatter fusion | flops 393217 | bytes 1573888
  563.0 1.9 collective-permute-start.3
  565.0 4.0 collective-permute-done.3
  569.3 1.3 stack.8
  570.6 18.0 %all-to-all-start.2 = ((f32[16,90,256]{2,1,0:T(8,128)}), f32[16,90,256]{2,1,0:T(8,128)S(1)}, u32[]{:S(2)}, u32[]{:S(2)}) async-start(f32[16,90,256]{2,1,0:T(8,128)} %stack.8), calls=%async_computation.2 | async-start | bytes 3145728 | tf_op jit(solution)/shard_map/all_to_all | solution.py:47
  588.5 0.5 all-reduce.17.cloned.1.call-start
  589.1 34.6 %all-to-all-done.2 = f32[16,90,256]{2,1,0:T(8,128)S(1)} async-done(((f32[16,90,256]{2,1,0:T(8,128)}), f32[16,90,256]{2,1,0:T(8,128)S(1)}, u32[]{:S(2)}, u32[]{:S(2)}) %all-to-all-start.2) | async-done | bytes 1474592 | tf_op jit(solution)/shard_map/all_to_all | solution.py:47
  623.9 19.0 %fusion.36 = f32[1440,256]{1,0:T(8,128)} fusion(f32[1440,256]{1,0:T(8,128)S(1)} %reshape.55, f32[1440,1440]{1,0:T(8,128)} %param.5, f32[]{:T(128)} %bitcast.1, s32[1440]{0:T(1024)S(1)} %get-tuple-element.45, s32[1440]{0:T(1024)S(1)} %get-tuple-element.46), kind=kOutput, calls=%fused_computation.66 | convolution fusion | flops 6376320000 | bytes 11255044 | tf_op jit(solution)/shard_map/dot_general | solution.py:32
  643.0 0.8 fusion.8
  643.8 75.7 %fusion.41 = (f32[96,256]{1,0:T(8,128)S(1)}, f32[96,256]{1,0:T(8,128)S(1)}) fusion(f32[1440,256]{1,0:T(8,128)} %fusion.36, f32[1440,256]{1,0:T(8,128)S(1)} %fusion.8), kind=kCustom, calls=%all-reduce-scatter.6 | all-reduce-scatter fusion | flops 786433 | bytes 3146752
  719.5 1.3 collective-permute-start.4
  720.8 1.5 collective-permute-start.5
  722.3 0.7 collective-permute-done.4
  723.3 1.1 fusion.21
  724.4 0.3 concatenate.12
  724.6 1.1 fusion.14
  725.8 257.5 %all-reduce.17.cloned.1.call-done = (f32[256,256]{0,1:T(8,128)}, f32[256,256]{0,1:T(8,128)}) async-done(((f32[256,256]{0,1:T(8,128)}, f32[256,256]{0,1:T(8,128)}), (f32[256,256]{0,1:T(8,128)}, f32[256,256]{0,1:T(8,128)})) %all-reduce.17.cloned.1.call-update) | async-done | bytes 524304 | tf_op jit(solution)/shard_map/psum | solution.py:88
  983.3 1.1 copy.16
  984.3 1.1 bitcast_add_fusion.1
  985.6 11.7 %cholesky.50 = f32[128,128]{1,0:T(8,128)S(1)} custom-call(f32[128,128]{1,0:T(8,128)S(1)} %cholesky.118), custom_call_target="Cholesky" | custom-call | tf_op jit(solution)/shard_map/jit(cholesky)/cholesky | solution.py:91
  997.4 9.8 custom-call.14
  1007.4 0.3 convolution_subtract_fusion.2
  1007.7 11.7 %cholesky.105 = f32[128,128]{1,0:T(8,128)S(1)} custom-call(f32[128,128]{1,0:T(8,128)S(1)} %convolution_subtract_fusion.2), custom_call_target="Cholesky" | custom-call | tf_op jit(solution)/shard_map/jit(cholesky)/cholesky | solution.py:91
  1019.4 0.6 compare_reduce_fusion
  1020.1 0.6 compare_reduce_fusion.1
  1022.0 3.8 while.4
  1022.0 0.6 fusion.56
  1022.6 1.3 bitcast_dynamic-update-slice_fusion.2
  1024.0 0.6 fusion.56
  1024.5 1.3 bitcast_dynamic-update-slice_fusion.2
  1025.8 19.9 %custom-call.17 = f32[2,128,128]{1,2,0:T(8,128)S(1)} custom-call(f32[2,128,128]{2,1,0:T(8,128)S(1)} %get-tuple-element.18), custom_call_target="InvertDiagBlocksLowerTriangular" | custom-call | tf_op jit(solution)/shard_map/jit(_solve_triangular)/triangular_solve | solution.py:93
  1045.9 0.3 fusion.12
  1046.2 0.3 convolution_subtract_fusion.1
  1046.5 0.3 fusion.27
  1046.9 0.3 fusion.10
  1047.2 0.4 convolution_subtract_fusion
  1047.6 0.3 fusion.26
  1047.9 0.7 pad_maximum_fusion
  (52 shorter events, 3.0 us)
Async XLA Ops:
  9.4 11.7 %copy-start.2 = (f32[2]{0:T(128)S(1)}, f32[2]{0:T(128)}, u32[]{:S(2)}) copy-start(f32[2]{0:T(128)} %param.7) | copy-start | bytes 28
  9.4 34.7 %all-to-all-start = ((f32[16,90,256]{2,1,0:T(8,128)}), f32[16,90,256]{2,1,0:T(8,128)S(1)}, u32[]{:S(2)}, u32[]{:S(2)}) async-start(f32[16,90,256]{2,1,0:T(8,128)} %stack.6), calls=%async_computation | async-start | bytes 3145728 | tf_op jit(solution)/shard_map/all_to_all | solution.py:47
  21.0 200.1 %all-gather.5.cloned.1.call-start = ((), (), s32[]{:S(2)}) async-start(), calls=%async_computation.3 | async-start | bytes 1671168 | tf_op jit(solution)/shard_map/all_gather | solution.py:51
  62.1 72.3 %copy-start.4 = (u32[256]{0:T(256)S(1)}, u32[256]{0:T(256)}, u32[]{:S(2)}) copy-start(u32[256]{0:T(256)} %constant.130) | copy-start | bytes 3076
  131.8 3.9 collective-permute-start
  136.6 366.8 %all-gather.7.cloned.1.call-start = ((), (), s32[]{:S(2)}) async-start(), calls=%async_computation.4 | async-start | bytes 1671168 | tf_op jit(solution)/shard_map/all_gather | solution.py:51
  232.7 50.1 %copy-start.3 = (u32[256]{0:T(256)S(1)}, u32[256]{0:T(256)}, u32[]{:S(2)}) copy-start(u32[256]{0:T(256)} %constant.134) | copy-start | bytes 3076
  232.7 54.3 %copy-start = (f32[90,256]{1,0:T(8,128)S(1)}, f32[90,256]{1,0:T(8,128)}, u32[]{:S(2)}) copy-start(f32[90,256]{1,0:T(8,128)} %param.6) | copy-start | bytes 276484
  280.8 5.9 collective-permute-start.1
  413.0 3.5 collective-permute-start.2
  563.0 5.9 collective-permute-start.3
  569.3 1.3 copy-start.1
  570.6 53.1 %all-to-all-start.2 = ((f32[16,90,256]{2,1,0:T(8,128)}), f32[16,90,256]{2,1,0:T(8,128)S(1)}, u32[]{:S(2)}, u32[]{:S(2)}) async-start(f32[16,90,256]{2,1,0:T(8,128)} %stack.8), calls=%async_computation.2 | async-start | bytes 3145728 | tf_op jit(solution)/shard_map/all_to_all | solution.py:47
  588.5 394.7 %all-reduce.17.cloned.1.call-start = ((), (), s32[]{:S(2)}) async-start(), calls=%async_computation.5 | async-start | bytes 1048576 | tf_op jit(solution)/shard_map/psum | solution.py:88
  719.5 3.5 collective-permute-start.4
  720.8 3.5 collective-permute-start.5
Sparse Core Ops, SparseCore 0:
  136.8 84.2 all-gather.4
  417.5 85.8 all-gather.6
  725.9 257.3 all-reduce.16
